TPU v7x, 32 devices: a whole 2x2x4 slice. The times are simulated.
32 devices in a mesh: groups: 2 (over y), ctx: 4 (over z), enc: 2 (over x), tp: 2 (over core).
Axes of the slice: x: 2, y: 2, z: 4, core: 2. Of those that a mesh axis runs over, the one named last changes fastest.
Arguments:
- enc_rows: bfloat16 [4, 1024, 1280], P(('groups', 'enc'), 'ctx'), parts along dimension 0, may hold values from -6 to 6
- row_slot: int32 [4, 1024], P(('groups', 'enc'), 'ctx'), parts along dimension 0, may hold values from 0 to 1023, as said below
- row_kind: int32 [4, 1024], P(('groups', 'enc'), 'ctx'), parts along dimension 0, may hold values from 0 to 1, as said below
- audio_proj: bfloat16 [1280, 8192], P(None, ('ctx', 'tp')), may hold values from -0.15625 to 0.15625
- frame_proj: bfloat16 [1280, 8192], P(None, ('ctx', 'tp')), may hold values from -0.15625 to 0.15625
- audio_bias: bfloat16 [8192], P(('ctx', 'tp')), may hold values from -3 to 3
- frame_bias: bfloat16 [8192], P(('ctx', 'tp')), may hold values from -3 to 3
- norm_gain: bfloat16 [8192], replicated, may hold values from 0.5 to 1.5
Outputs:
- normed: bfloat16 [4, 1024, 8192], P(('groups', 'enc'), ('ctx', 'tp')), parts along dimension 0
There are 2 independent parts, one for each index of `groups`. A program takes and returns all parts, laid end to end along the dimension named above; an argument that names none is the same for every part. Nothing has to cross between parts.
Inputs may be any that keep to these rules, and one draw needn't show every extreme that they name: `row_slot`: in each conversation every value appears exactly once. A row with value s fills context shard s // 256. Of the 256 rows of one owner (one index of ctx, in one conversation), at most 128 fill any one context shard, and every owner sends exactly 128 rows to some context shard. Rows come in 2-second spans of at most 128 rows: one span's rows are consecutive at the owner and fill consecutive positions. `row_kind`: within a span the audio rows come before the frame rows.
All inputs are finite; a program needn't handle non-finite values.
Results may differ from a plain program's by a relative error of at most 0.005.
Values may be sent and summed in bfloat16 or wider, within the bound.
No kernel may reach another device: no remote copies, remote signals or barrier semaphores. Data moves between devices by JAX's collectives and lax.ppermute only.
A program may use at most 128 MiB of HBM per device.

v0:
```python
import jax
import jax.numpy as jnp
from jax import lax
from jax.sharding import PartitionSpec as P


def project(enc_part, kind_part, weights, bias_audio, bias_frame):
    is_audio = (kind_part == 0)[:, None]
    nothing = jnp.zeros((), enc_part.dtype)
    stacked = jnp.concatenate(
        [jnp.where(is_audio, enc_part, nothing), jnp.where(is_audio, nothing, enc_part)], axis=1
    )
    result = jnp.dot(stacked, weights, preferred_element_type=jnp.float32)
    return result + jnp.where(is_audio, bias_audio[None, :], bias_frame[None, :])


def body(enc_rows, row_slot, row_kind, audio_proj, frame_proj, audio_bias, frame_bias, norm_gain):
    owned_rows = enc_rows[0]
    owned_slot = row_slot[0]
    owned_kind = row_kind[0]
    seq_dev = owned_rows.shape[0]
    width_enc = owned_rows.shape[1]
    n_ctx = lax.axis_size("ctx")
    capacity = 2 * seq_dev // n_ctx
    target = owned_slot // seq_dev
    position = owned_slot % seq_dev
    onehot = (target[:, None] == jnp.arange(n_ctx, dtype=jnp.int32)[None, :]).astype(jnp.int32)
    before = jnp.cumsum(onehot, axis=0) - onehot
    ranking = jnp.sum(before * onehot, axis=1)
    send_index = target * capacity + ranking
    outgoing = n_ctx * capacity
    select_send = send_index[None, :] == jnp.arange(outgoing, dtype=jnp.int32)[:, None]
    parcel = jnp.dot(
        select_send.astype(jnp.bfloat16), owned_rows, preferred_element_type=jnp.float32
    )
    parcel = parcel.astype(jnp.bfloat16).reshape(n_ctx, capacity, width_enc)
    send_int = select_send.astype(jnp.int32)
    where_to = (jnp.sum(send_int * (position + 1)[None, :], axis=1) - 1).reshape(n_ctx, capacity)
    what_kind = jnp.sum(send_int * owned_kind[None, :], axis=1).reshape(n_ctx, capacity)
    arrived = (
        lax.all_to_all(parcel, "ctx", split_axis=0, concat_axis=0, tiled=True),
        lax.all_to_all(where_to, "ctx", split_axis=0, concat_axis=0, tiled=True),
        lax.all_to_all(what_kind, "ctx", split_axis=0, concat_axis=0, tiled=True),
    )
    rows_in = arrived[0].reshape(outgoing, width_enc)
    pos_in = arrived[1].reshape(outgoing)
    kind_in = arrived[2].reshape(outgoing)
    select_land = pos_in[None, :] == jnp.arange(seq_dev, dtype=jnp.int32)[:, None]
    shard_rows = jnp.dot(
        select_land.astype(jnp.bfloat16), rows_in, preferred_element_type=jnp.float32
    ).astype(jnp.bfloat16)
    shard_kind = jnp.sum(select_land.astype(jnp.int32) * kind_in[None, :], axis=1)
    weights = jnp.concatenate([audio_proj, frame_proj], axis=0)
    bias_audio = audio_bias.astype(jnp.float32)
    bias_frame = frame_bias.astype(jnp.float32)
    columns = project(
        lax.all_gather(shard_rows, "ctx", axis=0, tiled=True),
        lax.all_gather(shard_kind, "ctx", axis=0, tiled=True),
        weights,
        bias_audio,
        bias_frame,
    )
    embeds = lax.all_to_all(
        columns.astype(jnp.bfloat16), ("ctx", "tp"), split_axis=0, concat_axis=1, tiled=True
    )
    widened = embeds.astype(jnp.float32)
    mean_square = jnp.mean(widened * widened, axis=-1, keepdims=True)
    normed = (widened * lax.rsqrt(mean_square + 1e-06) * norm_gain.astype(jnp.float32)).astype(
        jnp.bfloat16
    )
    return normed[None]


def solution(mesh):
    return jax.shard_map(
        body,
        mesh=mesh,
        in_specs=(
            P(("groups", "enc"), "ctx", None),
            P(("groups", "enc"), "ctx"),
            P(("groups", "enc"), "ctx"),
            P(None, ("ctx", "tp")),
            P(None, ("ctx", "tp")),
            P(("ctx", "tp")),
            P(("ctx", "tp")),
            P(),
        ),
        out_specs=P(("groups", "enc"), ("ctx", "tp"), None),
        check_vma=False,
    )
```

profile of v0, /device:TPU:0, one launch (start us, length us, event | category | flops | bytes accessed | tf_op | source)
XLA Modules:
  0.0 195.7 jit_solution(15758488479154289342)
XLA Ops:
  6.5 0.0 copy-start
  6.5 0.8 and_select_fusion.3
  7.3 0.7 and_select_fusion.2
  8.0 1.2 reduce-window.6
  9.2 0.1 slice.8
  9.3 0.1 copy.18
  9.4 0.1 copy.19
  9.5 0.1 add_bitcast_fusion
  9.6 0.7 multiply_add_fusion
  10.3 1.5 select_reduce_fusion.2
  11.8 0.6 broadcast_add_fusion
  12.4 6.3 %all-to-all-start = ((s32[4,1,128]{2,1,0:T(1,128)}), s32[4,1,128]{2,1,0:T(1,128)S(1)}, u32[]{:S(2)}, u32[]{:S(2)}) async-start(s32[4,1,128]{2,1,0:T(1,128)} %bitcast.7), calls=%async_computation | async-start | bytes 4096 | tf_op jit(solution)/shard_map/all_to_all | solution.py:42
  18.7 0.0 all-gather.3.cloned.1.call-start
  18.7 0.0 copy-done
  18.7 0.5 convolution_convert_fusion
  19.2 4.9 %all-to-all-done = s32[4,1,128]{2,1,0:T(1,128)S(1)} async-done(((s32[4,1,128]{2,1,0:T(1,128)}), s32[4,1,128]{2,1,0:T(1,128)S(1)}, u32[]{:S(2)}, u32[]{:S(2)}) %all-to-all-start) | async-done | bytes 2080 | tf_op jit(solution)/shard_map/all_to_all | solution.py:42
  24.2 0.0 copy-start.2
  24.2 0.0 copy-start.3
  24.2 32.7 %all_to_all.33 = bf16[4,128,1280]{2,1,0:T(8,128)(2,1)S(1)} all-to-all(bf16[4,128,1280]{2,1,0:T(8,128)(2,1)S(1)} %bitcast.39), channel_id=1, replica_groups=mesh['groups'=2,'ctx'=4,'enc'=2,'tp'=2] {'ctx'}, dimensions={0} | all-to-all | bytes 2621440 | tf_op jit(solution)/shard_map/all_to_all | solution.py:41
  56.9 1.3 convolution_convert_fusion.1
  58.3 0.0 all-gather.3.cloned.1.call-update
  58.3 3.2 %all-to-all-start.1 = ((s32[4,1,128]{2,1,0:T(1,128)}), s32[4,1,128]{2,1,0:T(1,128)S(1)}, u32[]{:S(2)}, u32[]{:S(2)}) async-start(s32[4,1,128]{2,1,0:T(1,128)} %bitcast.10), calls=%async_computation.1 | async-start | bytes 4096 | tf_op jit(solution)/shard_map/all_to_all | solution.py:43
  61.5 0.0 copy-done.2
  61.5 0.0 copy-done.3
  61.6 5.5 %all-to-all-done.1 = s32[4,1,128]{2,1,0:T(1,128)S(1)} async-done(((s32[4,1,128]{2,1,0:T(1,128)}), s32[4,1,128]{2,1,0:T(1,128)S(1)}, u32[]{:S(2)}, u32[]{:S(2)}) %all-to-all-start.1) | async-done | bytes 2080 | tf_op jit(solution)/shard_map/all_to_all | solution.py:43
  67.0 0.1 select_reduce_fusion
  67.2 8.4 %all-gather = s32[4,1,256]{2,1,0:T(1,128)S(1)} all-gather(s32[1,1,256]{2,1,0:T(1,128)S(1)} %bitcast.50), channel_id=1, replica_groups=mesh['groups'=2,'ctx'=4,'enc'=2,'tp'=2] {'ctx'}, dimensions={0}, use_global_device_ids=true | all-gather | bytes 5120 | tf_op jit(solution)/shard_map/all_gather | solution.py:58
  75.5 0.0 copy-start.4
  75.6 36.9 %all-gather.3.cloned.1.call-done = bf16[1024,1280]{1,0:T(8,128)(2,1)} async-done(((bf16[256,1280]{1,0:T(8,128)(2,1)}), bf16[1024,1280]{1,0:T(8,128)(2,1)}) %all-gather.3.cloned.1.call-update) | async-done | bytes 2621456 | tf_op jit(solution)/shard_map/all_gather | solution.py:57
  112.4 0.0 copy-start.5
  112.4 2.4 %broadcast_select_fusion.1 = (bf16[1024,1280]{1,0:T(8,128)(2,1)S(1)}, bf16[1024,1280]{1,0:T(8,128)(2,1)S(1)}) fusion(bf16[1024,1280]{1,0:T(8,128)(2,1)} %all-gather.3.cloned.1.call-done, pred[1024]{0:T(1024)(128)(4,1)S(1)} %reshape.162), kind=kLoop, calls=%fused_computation.14 | loop fusion | flops 2621440 | bytes 7865344 | tf_op jit(solution)/shard_map/jit(_where)/select_n | solution.py:11
  114.8 0.0 copy-done.4
  114.8 0.1 copy-done.5
  114.9 6.9 %add_convert_fusion = bf16[1024,1024]{1,0:T(8,128)(2,1)} fusion(f32[1024]{0:T(1024)S(1)} %convert_element_type.64, f32[1024]{0:T(1024)S(1)} %convert_element_type.63, pred[1024]{0:T(1024)(128)(4,1)S(1)} %reshape.162, bf16[1280,1024]{1,0:T(8,128)(2,1)S(1)} %copy-done.4, bf16[1280,1024]{1,0:T(8,128)(2,1)S(1)} %copy-done.5, ...), kind=kOutput, calls=%fused_computation.11 | convolution fusion | flops 5392826368 | bytes 12592128 | tf_op jit(solution)/shard_map/dot_general | solution.py:13
  121.8 0.0 copy-start.1
  121.8 3.7 %all-to-all-start.3 = ((bf16[8,128,1024]{2,1,0:T(8,128)(2,1)}), bf16[8,128,1024]{2,1,0:T(8,128)(2,1)S(1)}, u32[]{:S(2)}, u32[]{:S(2)}) async-start(bf16[8,128,1024]{2,1,0:T(8,128)(2,1)} %bitcast.41), calls=%async_computation.3 | async-start | bytes 4194304 | tf_op jit(solution)/shard_map/all_to_all | solution.py:63
  125.6 0.0 copy-done.1
  125.6 49.0 %all-to-all-done.3 = bf16[8,128,1024]{2,1,0:T(8,128)(2,1)S(1)} async-done(((bf16[8,128,1024]{2,1,0:T(8,128)(2,1)}), bf16[8,128,1024]{2,1,0:T(8,128)(2,1)S(1)}, u32[]{:S(2)}, u32[]{:S(2)}) %all-to-all-start.3) | async-done | bytes 2097184 | tf_op jit(solution)/shard_map/all_to_all | solution.py:63
  174.6 0.5 fusion.7
  175.1 0.5 convert_bitcast_fusion
  175.5 4.4 %copy.20 = f32[128,8,1024]{2,1,0:T(8,128)} copy(f32[128,8,1024]{2,0,1:T(8,128)S(1)} %convert_bitcast_fusion) | data formatting | bytes 8388608 | tf_op jit(solution)/shard_map/convert_element_type | solution.py:66
  179.9 5.0 %reshape.158 = f32[1,128,8192]{2,1,0:T(8,128)} reshape(f32[128,8,1024]{2,1,0:T(8,128)} %copy.20) | data formatting | bytes 8388608 | tf_op jit(solution)/shard_map/convert_element_type | solution.py:66
  184.9 4.0 %multiply_convert_fusion = bf16[1,128,8192]{2,1,0:T(8,128)(2,1)} fusion(f32[1,128,8192]{2,1,0:T(8,128)} %reshape.158, f32[8192]{0:T(1024)S(1)} %convert_element_type.70, f32[128]{0:T(128)S(1)} %add_rsqrt_fusion), kind=kLoop, calls=%fused_computation.10 | loop fusion | flops 3145728 | bytes 6324736 | tf_op jit(solution)/shard_map/convert_element_type | solution.py:68
  (10 shorter events, 0.1 us)
Async XLA Ops:
  6.5 12.2 %copy-start = (bf16[1,256,1280]{2,1,0:T(8,128)(2,1)S(1)}, bf16[1,256,1280]{2,1,0:T(8,128)(2,1)}, u32[]{:S(2)}) copy-start(bf16[1,256,1280]{2,1,0:T(8,128)(2,1)} %param.8) | copy-start | bytes 1966084
  12.4 11.8 %all-to-all-start = ((s32[4,1,128]{2,1,0:T(1,128)}), s32[4,1,128]{2,1,0:T(1,128)S(1)}, u32[]{:S(2)}, u32[]{:S(2)}) async-start(s32[4,1,128]{2,1,0:T(1,128)} %bitcast.7), calls=%async_computation | async-start | bytes 4096 | tf_op jit(solution)/shard_map/all_to_all | solution.py:42
  18.7 93.7 %all-gather.3.cloned.1.call-start = ((), (), s32[]{:S(2)}) async-start(), calls=%async_computation.4 | async-start | bytes 3276800 | tf_op jit(solution)/shard_map/all_gather | solution.py:57
  24.2 37.3 %copy-start.2 = (bf16[1024]{0:T(1024)(128)(2,1)S(1)}, bf16[1024]{0:T(1024)(128)(2,1)}, u32[]{:S(2)}) copy-start(bf16[1024]{0:T(1024)(128)(2,1)} %param.13) | copy-start | bytes 6148
  24.2 37.3 %copy-start.3 = (bf16[1024]{0:T(1024)(128)(2,1)S(1)}, bf16[1024]{0:T(1024)(128)(2,1)}, u32[]{:S(2)}) copy-start(bf16[1024]{0:T(1024)(128)(2,1)} %param.14) | copy-start | bytes 6148
  58.3 8.7 %all-to-all-start.1 = ((s32[4,1,128]{2,1,0:T(1,128)}), s32[4,1,128]{2,1,0:T(1,128)S(1)}, u32[]{:S(2)}, u32[]{:S(2)}) async-start(s32[4,1,128]{2,1,0:T(1,128)} %bitcast.10), calls=%async_computation.1 | async-start | bytes 4096 | tf_op jit(solution)/shard_map/all_to_all | solution.py:43
  75.5 39.2 %copy-start.4 = (bf16[1280,1024]{1,0:T(8,128)(2,1)S(1)}, bf16[1280,1024]{1,0:T(8,128)(2,1)}, u32[]{:S(2)}) copy-start(bf16[1280,1024]{1,0:T(8,128)(2,1)} %param.12) | copy-start | bytes 7864324
  112.4 2.5 %copy-start.5 = (bf16[1280,1024]{1,0:T(8,128)(2,1)S(1)}, bf16[1280,1024]{1,0:T(8,128)(2,1)}, u32[]{:S(2)}) copy-start(bf16[1280,1024]{1,0:T(8,128)(2,1)} %param.11) | copy-start | bytes 7864324
  121.8 3.7 %copy-start.1 = (bf16[8192]{0:T(1024)(128)(2,1)S(1)}, bf16[8192]{0:T(1024)(128)(2,1)}, u32[]{:S(2)}) copy-start(bf16[8192]{0:T(1024)(128)(2,1)} %param.15) | copy-start | bytes 49156
  121.8 52.7 %all-to-all-start.3 = ((bf16[8,128,1024]{2,1,0:T(8,128)(2,1)}), bf16[8,128,1024]{2,1,0:T(8,128)(2,1)S(1)}, u32[]{:S(2)}, u32[]{:S(2)}) async-start(bf16[8,128,1024]{2,1,0:T(8,128)(2,1)} %bitcast.41), calls=%async_computation.3 | async-start | bytes 4194304 | tf_op jit(solution)/shard_map/all_to_all | solution.py:63
Sparse Core Ops, SparseCore 0:
  58.4 53.9 all-gather.2
where the time goes:
time: 196 us
  waiting for transfers between devices  96.2 us (49%)
  blocking collectives  41.1 us (21%)
  between operations  13.5 us (7%)
  starting transfers between devices  13.2 us (7%)
  other arithmetic  13.1 us (7%)
  local copies, waits for them, and re-layouts  9.79 us (5%)
  matrix products  8.76 us (4%)
    all_to_all x1, waiting for transfers between devices, body(): lax.all_to_all(columns.astype(jnp.bfloat16), ('ctx', 'tp'), split_axis=0,...  49 us
    all_gather x1, waiting for transfers between devices, body(): lax.all_gather(shard_rows, 'ctx', axis=0, tiled=True)  36.9 us
    all_to_all x1, blocking collectives, body(): lax.all_to_all(parcel, 'ctx', split_axis=0, concat_axis=0, tiled=True)  32.7 us
    convert_element_type x2, local copies, waits for them, and re-layouts, body(): widened = embeds.astype(jnp.float32)  9.33 us
    all_gather x1, blocking collectives, body(): lax.all_gather(shard_kind, 'ctx', axis=0, tiled=True)  8.35 us
    dot_general x1, matrix products, project(): result = jnp.dot(stacked, weights, preferred_element_type=jnp.float32)  6.9 us
    all_to_all x1, starting transfers between devices, body(): lax.all_to_all(where_to, 'ctx', split_axis=0, concat_axis=0, tiled=True)  6.32 us
    all_to_all x1, waiting for transfers between devices, body(): lax.all_to_all(what_kind, 'ctx', split_axis=0, concat_axis=0, tiled=True)  5.47 us
  transfers between devices with their start and end apart: 4, of which 4 were waited for; matrix products, arithmetic and copies ran while one was open for 0% of the time, Pallas kernels for 0%

commit v1 on v0

--- a/solution.py
+++ b/solution.py
@@ -37,8 +37,28 @@
     send_int = select_send.astype(jnp.int32)
     where_to = (jnp.sum(send_int * (position + 1)[None, :], axis=1) - 1).reshape(n_ctx, capacity)
     what_kind = jnp.sum(send_int * owned_kind[None, :], axis=1).reshape(n_ctx, capacity)
+
+    def produce_the_ports(local, which_dim, d0):
+        across = "ctx"
+        block_next = lax.axis_size(across)
+        frame_out = lax.axis_index(across)
+        reached, f_next = (block_next, frame_out)
+        finding = local.shape[which_dim] // reached
+        all_rows = jnp.roll(local, -f_next * finding, which_dim)
+        g_now = lax.slice_in_dim(all_rows, 0, finding, axis=which_dim)
+        copies = [g_now]
+        for nth in [*range(1, reached)]:
+            mid_arr = lax.slice_in_dim(all_rows, nth * finding, (nth + 1) * finding, axis=which_dim)
+            current_arr = lax.ppermute(
+                mid_arr, across, [(it, (it + nth) % reached) for it in range(reached)]
+            )
+            copies.append(current_arr)
+        passed = jnp.concatenate(copies[::-1], d0)
+        t_next = jnp.roll(passed, (f_next + 1) * copies[0].shape[d0], d0)
+        return t_next
+
     arrived = (
-        lax.all_to_all(parcel, "ctx", split_axis=0, concat_axis=0, tiled=True),
+        produce_the_ports(parcel, 0, 0),
         lax.all_to_all(where_to, "ctx", split_axis=0, concat_axis=0, tiled=True),
         lax.all_to_all(what_kind, "ctx", split_axis=0, concat_axis=0, tiled=True),
     )

time: 196 us -> 186 us (0.949)
  blocking collectives: 41.1 us -> 8.73 us
  waiting for transfers between devices: 96.2 us -> 112 us
  starting transfers between devices: 13.2 us -> 18.7 us
    all_to_all x1 -> x0, blocking collectives: 32.7 us -> none  [body(): lax.all_to_all(parcel, 'ctx', split_axis=0, concat_axis=0, tiled=True)]
    ppermute x0 -> x3, waiting for transfers between devices: none -> 15.3 us  [produce_the_ports(): lax.ppermute(mid_arr, across, [(it, (it + nth) % reached) for it in range...]
    ppermute x0 -> x3, starting transfers between devices: none -> 7.01 us  [produce_the_ports(): lax.ppermute(mid_arr, across, [(it, (it + nth) % reached) for it in range...]
    all_to_all x1, starting transfers between devices: 6.32 us -> 3.22 us  [body(): lax.all_to_all(where_to, 'ctx', split_axis=0, concat_axis=0, tiled=True)]
    concatenate x0 -> x2, other arithmetic: none -> 2.04 us  [the longest x1 1.55 us: produce_the_ports(): t_next = jnp.roll(passed, (f_next + 1) * copies[0].shape[d0], d0)]
  transfers between devices with their start and end apart: 4 -> 7, of which waited for: 4 -> 6; matrix products, arithmetic and copies ran while one was open for 0% -> 2% of each run, Pallas kernels for 0% -> 0%
where the time goes in v1:
time: 186 us
  waiting for transfers between devices  112 us (60%)
  starting transfers between devices  18.7 us (10%)
  other arithmetic  14.4 us (8%)
  between operations  13.6 us (7%)
  local copies, waits for them, and re-layouts  9.89 us (5%)
  matrix products  8.76 us (5%)
  blocking collectives  8.73 us (5%)
    all_to_all x1, waiting for transfers between devices, body(): lax.all_to_all(columns.astype(jnp.bfloat16), ('ctx', 'tp'), split_axis=0,...  48.8 us
    all_gather x1, waiting for transfers between devices, body(): lax.all_gather(shard_rows, 'ctx', axis=0, tiled=True)  36.8 us
    ppermute x3, waiting for transfers between devices, produce_the_ports(): lax.ppermute(mid_arr, across, [(it, (it + nth) % reached) for it in range...  15.3 us
    convert_element_type x2, local copies, waits for them, and re-layouts, body(): widened = embeds.astype(jnp.float32)  9.33 us
    all_gather x1, blocking collectives, body(): lax.all_gather(shard_kind, 'ctx', axis=0, tiled=True)  8.73 us
    ppermute x3, starting transfers between devices, produce_the_ports(): lax.ppermute(mid_arr, across, [(it, (it + nth) % reached) for it in range...  7.01 us
    dot_general x1, matrix products, project(): result = jnp.dot(stacked, weights, preferred_element_type=jnp.float32)  6.9 us
    all_to_all x1, waiting for transfers between devices, body(): lax.all_to_all(what_kind, 'ctx', split_axis=0, concat_axis=0, tiled=True)  5.52 us
  transfers between devices with their start and end apart: 7, of which 6 were waited for; matrix products, arithmetic and copies ran while one was open for 2% of the time, Pallas kernels for 0%

profile of v1, /device:TPU:0, one launch (start us, length us, event | category | flops | bytes accessed | tf_op | source)
XLA Modules:
  0.0 185.9 jit_solution(11107481050012932330)
XLA Ops:
  6.5 0.0 copy-start
  6.5 0.8 and_select_fusion.3
  7.3 0.7 and_select_fusion.2
  8.0 1.2 reduce-window.6
  9.2 0.1 slice.24
  9.3 0.1 copy.18
  9.4 0.1 copy.19
  9.5 0.1 add_bitcast_fusion
  9.6 0.7 multiply_add_fusion
  10.3 0.0 copy-done
  10.3 0.5 convolution_convert_fusion
  10.9 0.0 copy-start.4
  10.9 0.5 fusion.19
  11.4 0.1 fusion.28
  11.5 3.1 %collective-permute-start.2 = (bf16[1,128,1280]{2,1,0:T(8,128)(2,1)S(1)}, bf16[1,128,1280]{2,1,0:T(8,128)(2,1)S(1)}, u32[]{:S(2)}, u32[]{:S(2)}) collective-permute-start(bf16[1,128,1280]{2,1,0:T(8,128)(2,1)S(1)} %get-tuple-element.11), channel_id=1, source_target_pairs={{0,4},{4,8},{8,12},{12,0},{1,5},{5,9},{9,13},{13,1},{2,6},{6,10},{... | collective-permute-start | bytes 983048 | tf_op jit(solution)/shard_map/ppermute | solution.py:52
  14.5 2.6 %collective-permute-start.1 = (bf16[1,128,1280]{2,1,0:T(8,128)(2,1)S(1)}, bf16[1,128,1280]{2,1,0:T(8,128)(2,1)S(1)}, u32[]{:S(2)}, u32[]{:S(2)}) collective-permute-start(bf16[1,128,1280]{2,1,0:T(8,128)(2,1)S(1)} %get-tuple-element.12), channel_id=1, source_target_pairs={{0,8},{4,12},{8,0},{12,4},{1,9},{5,13},{9,1},{13,5},{2,10},{6,14},... | collective-permute-start | bytes 983048 | tf_op jit(solution)/shard_map/ppermute | solution.py:52
  17.1 1.3 collective-permute-start
  18.5 0.0 copy-done.4
  18.5 0.8 select_reduce_fusion.2
  19.3 0.6 broadcast_add_fusion
  19.9 3.2 %all-to-all-start = ((s32[4,1,128]{2,1,0:T(1,128)}), s32[4,1,128]{2,1,0:T(1,128)S(1)}, u32[]{:S(2)}, u32[]{:S(2)}) async-start(s32[4,1,128]{2,1,0:T(1,128)} %bitcast.7), calls=%async_computation | async-start | bytes 4096 | tf_op jit(solution)/shard_map/all_to_all | solution.py:62
  23.1 0.0 all-gather.3.cloned.1.call-start
  23.2 2.1 %collective-permute-done.2 = bf16[1,128,1280]{2,1,0:T(8,128)(2,1)S(1)} collective-permute-done((bf16[1,128,1280]{2,1,0:T(8,128)(2,1)S(1)}, bf16[1,128,1280]{2,1,0:T(8,128)(2,1)S(1)}, u32[]{:S(2)}, u32[]{:S(2)}) %collective-permute-start.2) | collective-permute-done | bytes 327712 | tf_op jit(solution)/shard_map/ppermute | solution.py:52
  25.2 13.2 %collective-permute-done.1 = bf16[1,128,1280]{2,1,0:T(8,128)(2,1)S(1)} collective-permute-done((bf16[1,128,1280]{2,1,0:T(8,128)(2,1)S(1)}, bf16[1,128,1280]{2,1,0:T(8,128)(2,1)S(1)}, u32[]{:S(2)}, u32[]{:S(2)}) %collective-permute-start.1) | collective-permute-done | bytes 327712 | tf_op jit(solution)/shard_map/ppermute | solution.py:52
  38.5 0.0 collective-permute-done
  38.5 1.6 fusion.15
  40.0 5.4 %all-to-all-done = s32[4,1,128]{2,1,0:T(1,128)S(1)} async-done(((s32[4,1,128]{2,1,0:T(1,128)}), s32[4,1,128]{2,1,0:T(1,128)S(1)}, u32[]{:S(2)}, u32[]{:S(2)}) %all-to-all-start) | async-done | bytes 2080 | tf_op jit(solution)/shard_map/all_to_all | solution.py:62
  45.4 1.3 convolution_convert_fusion.1
  46.7 0.0 all-gather.3.cloned.1.call-update
  46.8 4.5 %all-to-all-start.1 = ((s32[4,1,128]{2,1,0:T(1,128)}), s32[4,1,128]{2,1,0:T(1,128)S(1)}, u32[]{:S(2)}, u32[]{:S(2)}) async-start(s32[4,1,128]{2,1,0:T(1,128)} %bitcast.10), calls=%async_computation.1 | async-start | bytes 4096 | tf_op jit(solution)/shard_map/all_to_all | solution.py:63
  51.3 0.0 copy-done.2
  51.3 0.0 copy-done.3
  51.3 5.5 %all-to-all-done.1 = s32[4,1,128]{2,1,0:T(1,128)S(1)} async-done(((s32[4,1,128]{2,1,0:T(1,128)}), s32[4,1,128]{2,1,0:T(1,128)S(1)}, u32[]{:S(2)}, u32[]{:S(2)}) %all-to-all-start.1) | async-done | bytes 2080 | tf_op jit(solution)/shard_map/all_to_all | solution.py:63
  56.8 0.1 select_reduce_fusion
  56.9 8.7 %all-gather = s32[4,1,256]{2,1,0:T(1,128)S(1)} all-gather(s32[1,1,256]{2,1,0:T(1,128)S(1)} %bitcast.49), channel_id=1, replica_groups=mesh['groups'=2,'ctx'=4,'enc'=2,'tp'=2] {'ctx'}, dimensions={0}, use_global_device_ids=true | all-gather | bytes 5120 | tf_op jit(solution)/shard_map/all_gather | solution.py:78
  65.7 36.8 %all-gather.3.cloned.1.call-done = bf16[1024,1280]{1,0:T(8,128)(2,1)} async-done(((bf16[256,1280]{1,0:T(8,128)(2,1)}), bf16[1024,1280]{1,0:T(8,128)(2,1)}) %all-gather.3.cloned.1.call-update) | async-done | bytes 2621456 | tf_op jit(solution)/shard_map/all_gather | solution.py:77
  102.6 2.4 %broadcast_select_fusion.1 = (bf16[1024,1280]{1,0:T(8,128)(2,1)S(1)}, bf16[1024,1280]{1,0:T(8,128)(2,1)S(1)}) fusion(bf16[1024,1280]{1,0:T(8,128)(2,1)} %all-gather.3.cloned.1.call-done, pred[1024]{0:T(1024)(128)(4,1)S(1)} %reshape.162), kind=kLoop, calls=%fused_computation.24 | loop fusion | flops 2621440 | bytes 7865344 | tf_op jit(solution)/shard_map/jit(_where)/select_n | solution.py:11
  104.9 0.0 copy-done.5
  104.9 0.1 copy-done.6
  105.1 6.9 %add_convert_fusion = bf16[1024,1024]{1,0:T(8,128)(2,1)} fusion(f32[1024]{0:T(1024)S(1)} %convert_element_type.64, f32[1024]{0:T(1024)S(1)} %convert_element_type.63, pred[1024]{0:T(1024)(128)(4,1)S(1)} %reshape.162, bf16[1280,1024]{1,0:T(8,128)(2,1)S(1)} %copy-done.5, bf16[1280,1024]{1,0:T(8,128)(2,1)S(1)} %copy-done.6, ...), kind=kOutput, calls=%fused_computation.11 | convolution fusion | flops 5392826368 | bytes 12592128 | tf_op jit(solution)/shard_map/dot_general | solution.py:13
  112.0 3.9 %all-to-all-start.2 = ((bf16[8,128,1024]{2,1,0:T(8,128)(2,1)}), bf16[8,128,1024]{2,1,0:T(8,128)(2,1)S(1)}, u32[]{:S(2)}, u32[]{:S(2)}) async-start(bf16[8,128,1024]{2,1,0:T(8,128)(2,1)} %bitcast.41), calls=%async_computation.2 | async-start | bytes 4194304 | tf_op jit(solution)/shard_map/all_to_all | solution.py:83
  115.9 0.0 copy-done.1
  115.9 48.8 %all-to-all-done.2 = bf16[8,128,1024]{2,1,0:T(8,128)(2,1)S(1)} async-done(((bf16[8,128,1024]{2,1,0:T(8,128)(2,1)}), bf16[8,128,1024]{2,1,0:T(8,128)(2,1)S(1)}, u32[]{:S(2)}, u32[]{:S(2)}) %all-to-all-start.2) | async-done | bytes 2097184 | tf_op jit(solution)/shard_map/all_to_all | solution.py:83
  164.7 0.5 fusion.7
  165.2 0.5 convert_bitcast_fusion
  165.7 4.4 %copy.20 = f32[128,8,1024]{2,1,0:T(8,128)} copy(f32[128,8,1024]{2,0,1:T(8,128)S(1)} %convert_bitcast_fusion) | data formatting | bytes 8388608 | tf_op jit(solution)/shard_map/convert_element_type | solution.py:86
  170.1 5.0 %reshape.158 = f32[1,128,8192]{2,1,0:T(8,128)} reshape(f32[128,8,1024]{2,1,0:T(8,128)} %copy.20) | data formatting | bytes 8388608 | tf_op jit(solution)/shard_map/convert_element_type | solution.py:86
  175.0 4.0 %multiply_convert_fusion = bf16[1,128,8192]{2,1,0:T(8,128)(2,1)} fusion(f32[1,128,8192]{2,1,0:T(8,128)} %reshape.158, f32[8192]{0:T(1024)S(1)} %convert_element_type.70, f32[128]{0:T(128)S(1)} %add_rsqrt_fusion), kind=kLoop, calls=%fused_computation.10 | loop fusion | flops 3145728 | bytes 6324736 | tf_op jit(solution)/shard_map/convert_element_type | solution.py:88
  (15 shorter events, 0.1 us)
Async XLA Ops:
  6.5 3.8 %copy-start = (bf16[1,256,1280]{2,1,0:T(8,128)(2,1)S(1)}, bf16[1,256,1280]{2,1,0:T(8,128)(2,1)}, u32[]{:S(2)}) copy-start(bf16[1,256,1280]{2,1,0:T(8,128)(2,1)} %param.10) | copy-start | bytes 1966084
  10.9 7.6 %copy-start.4 = (s32[1,256]{1,0:T(1,128)S(1)}, s32[1,256]{1,0:T(1,128)}, u32[]{:S(2)}) copy-start(s32[1,256]{1,0:T(1,128)} %param.12) | copy-start | bytes 3076
  11.5 13.8 %collective-permute-start.2 = (bf16[1,128,1280]{2,1,0:T(8,128)(2,1)S(1)}, bf16[1,128,1280]{2,1,0:T(8,128)(2,1)S(1)}, u32[]{:S(2)}, u32[]{:S(2)}) collective-permute-start(bf16[1,128,1280]{2,1,0:T(8,128)(2,1)S(1)} %get-tuple-element.11), channel_id=1, source_target_pairs={{0,4},{4,8},{8,12},{12,0},{1,5},{5,9},{9,13},{13,1},{2,6},{6,10},{... | collective-permute-start | bytes 983048 | tf_op jit(solution)/shard_map/ppermute | solution.py:52
  14.5 23.9 %collective-permute-start.1 = (bf16[1,128,1280]{2,1,0:T(8,128)(2,1)S(1)}, bf16[1,128,1280]{2,1,0:T(8,128)(2,1)S(1)}, u32[]{:S(2)}, u32[]{:S(2)}) collective-permute-start(bf16[1,128,1280]{2,1,0:T(8,128)(2,1)S(1)} %get-tuple-element.12), channel_id=1, source_target_pairs={{0,8},{4,12},{8,0},{12,4},{1,9},{5,13},{9,1},{13,5},{2,10},{6,14},... | collective-permute-start | bytes 983048 | tf_op jit(solution)/shard_map/ppermute | solution.py:52
  17.1 21.4 %collective-permute-start = (bf16[1,128,1280]{2,1,0:T(8,128)(2,1)S(1)}, bf16[1,128,1280]{2,1,0:T(8,128)(2,1)S(1)}, u32[]{:S(2)}, u32[]{:S(2)}) collective-permute-start(bf16[1,128,1280]{2,1,0:T(8,128)(2,1)S(1)} %get-tuple-element.13), channel_id=1, source_target_pairs={{0,12},{4,0},{8,4},{12,8},{1,13},{5,1},{9,5},{13,9},{2,14},{6,2},{... | collective-permute-start | bytes 983048 | tf_op jit(solution)/shard_map/ppermute | solution.py:52
  19.9 25.5 %all-to-all-start = ((s32[4,1,128]{2,1,0:T(1,128)}), s32[4,1,128]{2,1,0:T(1,128)S(1)}, u32[]{:S(2)}, u32[]{:S(2)}) async-start(s32[4,1,128]{2,1,0:T(1,128)} %bitcast.7), calls=%async_computation | async-start | bytes 4096 | tf_op jit(solution)/shard_map/all_to_all | solution.py:62
  23.1 79.4 %all-gather.3.cloned.1.call-start = ((), (), s32[]{:S(2)}) async-start(), calls=%async_computation.3 | async-start | bytes 3276800 | tf_op jit(solution)/shard_map/all_gather | solution.py:77
  38.5 12.8 %copy-start.2 = (bf16[1024]{0:T(1024)(128)(2,1)S(1)}, bf16[1024]{0:T(1024)(128)(2,1)}, u32[]{:S(2)}) copy-start(bf16[1024]{0:T(1024)(128)(2,1)} %param.15) | copy-start | bytes 6148
  38.5 12.8 %copy-start.3 = (bf16[1024]{0:T(1024)(128)(2,1)S(1)}, bf16[1024]{0:T(1024)(128)(2,1)}, u32[]{:S(2)}) copy-start(bf16[1024]{0:T(1024)(128)(2,1)} %param.16) | copy-start | bytes 6148
  46.8 10.0 %all-to-all-start.1 = ((s32[4,1,128]{2,1,0:T(1,128)}), s32[4,1,128]{2,1,0:T(1,128)S(1)}, u32[]{:S(2)}, u32[]{:S(2)}) async-start(s32[4,1,128]{2,1,0:T(1,128)} %bitcast.10), calls=%async_computation.1 | async-start | bytes 4096 | tf_op jit(solution)/shard_map/all_to_all | solution.py:63
  65.7 39.2 %copy-start.5 = (bf16[1280,1024]{1,0:T(8,128)(2,1)S(1)}, bf16[1280,1024]{1,0:T(8,128)(2,1)}, u32[]{:S(2)}) copy-start(bf16[1280,1024]{1,0:T(8,128)(2,1)} %param.14) | copy-start | bytes 7864324
  102.6 2.5 %copy-start.6 = (bf16[1280,1024]{1,0:T(8,128)(2,1)S(1)}, bf16[1280,1024]{1,0:T(8,128)(2,1)}, u32[]{:S(2)}) copy-start(bf16[1280,1024]{1,0:T(8,128)(2,1)} %param.13) | copy-start | bytes 7864324
  112.0 3.9 %copy-start.1 = (bf16[8192]{0:T(1024)(128)(2,1)S(1)}, bf16[8192]{0:T(1024)(128)(2,1)}, u32[]{:S(2)}) copy-start(bf16[8192]{0:T(1024)(128)(2,1)} %param.17) | copy-start | bytes 49156
  112.0 52.7 %all-to-all-start.2 = ((bf16[8,128,1024]{2,1,0:T(8,128)(2,1)}), bf16[8,128,1024]{2,1,0:T(8,128)(2,1)S(1)}, u32[]{:S(2)}, u32[]{:S(2)}) async-start(bf16[8,128,1024]{2,1,0:T(8,128)(2,1)} %bitcast.41), calls=%async_computation.2 | async-start | bytes 4194304 | tf_op jit(solution)/shard_map/all_to_all | solution.py:83
Sparse Core Ops, SparseCore 0:
  46.9 55.6 all-gather.2
